TPU v7x, 32 devices: a whole 2x2x4 slice. The times are simulated.
32 devices in a mesh: dp: 8 (over z, y), bfly: 4 (over x, core).
Axes of the slice: x: 2, y: 2, z: 4, core: 2. Of those that a mesh axis runs over, the one named last changes fastest.
Arguments:
- tokens: bfloat16 [2048, 12288], P('dp', 'bfly'), may hold values from -6 to 6
- grad_out: bfloat16 [2048, 12288], P('dp', 'bfly'), may hold values from -6 to 6
- weight_a: bfloat16 [48, 256, 512], P('bfly', 'dp'), may hold values from -0.375 to 0.375
- weight_b: bfloat16 [96, 256, 256], P('bfly', 'dp'), may hold values from -0.375 to 0.375
- weight_c: bfloat16 [96, 256, 256], P('bfly', 'dp'), may hold values from -0.375 to 0.375
- weight_e: bfloat16 [48, 512, 256], P('bfly', 'dp'), may hold values from -0.25 to 0.25
Outputs:
- output: bfloat16 [2048, 12288], P('dp', 'bfly')
- grad_in: bfloat16 [2048, 12288], P('dp', 'bfly')
- grad_a: float32 [48, 256, 512], P('bfly', 'dp')
- grad_b: float32 [96, 256, 256], P('bfly', 'dp')
- grad_c: float32 [96, 256, 256], P('bfly', 'dp')
- grad_e: float32 [48, 512, 256], P('bfly', 'dp')
All inputs are finite; a program needn't handle non-finite values.
Results may differ from a plain program's by a relative error of at most 0.03.
Values may be sent and summed in bfloat16 or wider, within the bound.
No kernel may reach another device: no remote copies, remote signals or barrier semaphores. Data moves between devices by JAX's collectives and lax.ppermute only.
A program may use at most 128 MiB of HBM per device.

v0:
```python
import jax
import jax.numpy as jnp
from jax import lax
from jax.sharding import PartitionSpec as P

BLK = 256
gelu_scale = 0.7978845608028654


def gelu_pair(hidden):
    inner_arg = gelu_scale * (hidden + 0.044715 * hidden * hidden * hidden)
    tangent = jnp.tanh(inner_arg)
    gelu_value = 0.5 * hidden * (1.0 + tangent)
    gelu_slope = 0.5 * (1.0 + tangent) + 0.5 * hidden * (1.0 - tangent * tangent) * gelu_scale * (
        1.0 + 3.0 * 0.044715 * hidden * hidden
    )
    return (gelu_value, gelu_slope)


def regroup(parcels, group_count, after_fns):
    parcel_count = len(parcels)
    local_blocks, block_width, token_count = parcels[0].shape
    sub_width = block_width // group_count
    stacked = jnp.stack(parcels, axis=0).reshape(
        parcel_count, local_blocks, group_count, sub_width, token_count
    )
    arrived = lax.all_to_all(stacked, "bfly", split_axis=2, concat_axis=2, tiled=True)
    flat_results = []
    piece = arrived[0].reshape(local_blocks, block_width, arrived.shape[4])
    flat_results.extend(after_fns[0](piece))
    return tuple(flat_results)


def per_device(tokens, grad_out, weight_a, weight_b, weight_c, weight_e):
    group_count = lax.axis_size("bfly")
    full_a, full_b, full_c, full_e = (
        lax.all_gather(weight_a, "dp", axis=1, tiled=True),
        lax.all_gather(weight_b, "dp", axis=1, tiled=True),
        lax.all_gather(weight_c, "dp", axis=1, tiled=True),
        lax.all_gather(weight_e, "dp", axis=1, tiled=True),
    )
    token_count = tokens.shape[0]
    inner_blocks = full_a.shape[0]
    spread_width = full_a.shape[2]
    local_blocks = full_b.shape[0]
    inputs = tokens.reshape(token_count, inner_blocks, BLK).transpose(1, 2, 0)
    upstream = grad_out.reshape(token_count, inner_blocks, BLK).transpose(1, 2, 0)
    spread = jnp.einsum("kit,kio->kot", inputs, full_a, preferred_element_type=jnp.float32)
    spread = spread.astype(jnp.bfloat16).reshape(local_blocks, BLK, token_count)
    back_out = jnp.einsum("kjt,koj->kot", upstream, full_e, preferred_element_type=jnp.float32)
    back_out = back_out.astype(jnp.bfloat16).reshape(local_blocks, BLK, token_count)

    def up_second(permuted):
        return (
            permuted,
            jnp.einsum("qit,qij->qjt", permuted, full_b, preferred_element_type=jnp.float32),
        )

    def back_second(back_mid):
        return (
            back_mid,
            jnp.einsum("qjt,qij->qit", back_mid, full_c, preferred_element_type=jnp.float32),
        )

    def down_second(returned):
        wide_view = returned.reshape(inner_blocks, spread_width, returned.shape[2])
        return (
            returned,
            jnp.einsum("kot,koj->kjt", wide_view, full_e, preferred_element_type=jnp.float32),
        )

    def back_last(back_spread):
        wide_view = back_spread.reshape(inner_blocks, spread_width, back_spread.shape[2])
        return (
            back_spread,
            jnp.einsum("kot,kio->kit", wide_view, full_a, preferred_element_type=jnp.float32),
        )

    permuted, hidden = regroup((spread,), group_count, (up_second,))
    gelu_value, gelu_slope = gelu_pair(hidden)
    active = gelu_value.astype(jnp.bfloat16)
    narrowed = jnp.einsum(
        "qit,qij->qjt", active, full_c, preferred_element_type=jnp.float32
    ).astype(jnp.bfloat16)
    returned, output = regroup((narrowed,), group_count, (down_second,))
    back_mid, back_act = regroup((back_out,), group_count, (back_second,))
    back_hidden = (back_act * gelu_slope).astype(jnp.bfloat16)
    back_first = jnp.einsum(
        "qjt,qij->qit", back_hidden, full_b, preferred_element_type=jnp.float32
    ).astype(jnp.bfloat16)
    back_spread, back_input = regroup((back_first,), group_count, (back_last,))
    spread_back = back_spread.reshape(inner_blocks, spread_width, token_count)
    returned_wide = returned.reshape(inner_blocks, spread_width, token_count)
    part_a = jnp.einsum("kit,kot->kio", inputs, spread_back, preferred_element_type=jnp.float32)
    part_b = jnp.einsum("qit,qjt->qij", permuted, back_hidden, preferred_element_type=jnp.float32)
    part_c = jnp.einsum("qit,qjt->qij", active, back_mid, preferred_element_type=jnp.float32)
    part_e = jnp.einsum("kot,kjt->koj", returned_wide, upstream, preferred_element_type=jnp.float32)
    grad_a, grad_b, grad_c, grad_e = (
        lax.psum_scatter(part_a.astype(jnp.bfloat16), "dp", scatter_dimension=1, tiled=True).astype(
            jnp.float32
        ),
        lax.psum_scatter(part_b.astype(jnp.bfloat16), "dp", scatter_dimension=1, tiled=True).astype(
            jnp.float32
        ),
        lax.psum_scatter(part_c.astype(jnp.bfloat16), "dp", scatter_dimension=1, tiled=True).astype(
            jnp.float32
        ),
        lax.psum_scatter(part_e.astype(jnp.bfloat16), "dp", scatter_dimension=1, tiled=True).astype(
            jnp.float32
        ),
    )
    output = output.astype(jnp.bfloat16).transpose(2, 0, 1).reshape(token_count, inner_blocks * BLK)
    grad_in = (
        back_input.astype(jnp.bfloat16).transpose(2, 0, 1).reshape(token_count, inner_blocks * BLK)
    )
    return (output, grad_in, grad_a, grad_b, grad_c, grad_e)


def solution(mesh):
    in_specs = (
        P("dp", "bfly"),
        P("dp", "bfly"),
        P("bfly", "dp", None),
        P("bfly", "dp", None),
        P("bfly", "dp", None),
        P("bfly", "dp", None),
    )
    out_specs = (
        P("dp", "bfly"),
        P("dp", "bfly"),
        P("bfly", "dp", None),
        P("bfly", "dp", None),
        P("bfly", "dp", None),
        P("bfly", "dp", None),
    )
    return jax.shard_map(
        per_device, mesh=mesh, in_specs=in_specs, out_specs=out_specs, check_vma=False
    )
```

profile of v0, /device:TPU:0, one launch (start us, length us, event | category | flops | bytes accessed | tf_op | source)
XLA Modules:
  0.0 599.6 jit_solution(6045464597825398712)
XLA Ops:
  11.7 61.7 %all-gather.5.cloned.1.call-done = bf16[12,256,512]{2,1,0:T(8,128)(2,1)} async-done(((bf16[12,32,512]{2,1,0:T(8,128)(2,1)}), bf16[12,256,512]{2,1,0:T(8,128)(2,1)}) %all-gather.5.cloned.1.call-update) | async-done | bytes 3145744 | tf_op jit(solution)/shard_map/all_gather | solution.py:37
  73.4 3.0 convolution_convert_fusion.2
  78.3 4.8 all-to-all-start
  83.9 50.9 %all-gather.11.cloned.1.call-done = bf16[12,512,256]{2,1,0:T(8,128)(2,1)} async-done(((bf16[12,64,256]{2,1,0:T(8,128)(2,1)}), bf16[12,512,256]{2,1,0:T(8,128)(2,1)}) %all-gather.11.cloned.1.call-update) | async-done | bytes 3145744 | tf_op jit(solution)/shard_map/all_gather | solution.py:40
  134.8 2.9 convolution_convert_fusion.1
  137.7 2.1 copy.44
  139.8 4.7 all-to-all-start.2
  144.5 2.1 copy.38
  146.6 34.8 %all-to-all-done.2 = bf16[1,24,4,64,256]{4,3,1,0,2:T(8,128)(2,1)} async-done(((bf16[1,24,4,64,256]{4,3,1,0,2:T(8,128)(2,1)}), bf16[1,24,4,64,256]{4,3,1,0,2:T(8,128)(2,1)}, u32[]{:S(2)}, u32[]{:S(2)}) %all-to-all-start.2) | async-done | bytes 3145760 | tf_op jit(solution)/shard_map/all_to_all | solution.py:27
  181.5 4.0 copy.45
  185.5 10.7 %all-gather.7.cloned.1.call-done = bf16[24,256,256]{2,1,0:T(8,128)(2,1)} async-done(((bf16[24,32,256]{2,1,0:T(8,128)(2,1)}), bf16[24,256,256]{2,1,0:T(8,128)(2,1)}) %all-gather.7.cloned.1.call-update) | async-done | bytes 3145744 | tf_op jit(solution)/shard_map/all_gather | solution.py:38
  196.1 5.6 fusion.7
  201.7 55.6 %all-gather.9.cloned.1.call-done = bf16[24,256,256]{2,1,0:T(8,128)(2,1)} async-done(((bf16[24,32,256]{2,1,0:T(8,128)(2,1)}), bf16[24,256,256]{2,1,0:T(8,128)(2,1)}) %all-gather.9.cloned.1.call-update) | async-done | bytes 3145744 | tf_op jit(solution)/shard_map/all_gather | solution.py:39
  257.4 8.4 %fusion.6 = bf16[24,256,256]{1,2,0:T(8,128)(2,1)S(1)} fusion(f32[24,256,256]{2,1,0:T(8,128)} %fusion.7, bf16[24,256,256]{2,1,0:T(8,128)(2,1)} %bitcast.79, bf16[24,256,256]{2,1,0:T(8,128)(2,1)} %all-gather.9.cloned.1.call-done), kind=kOutput, calls=%fused_computation.8 | convolution fusion | flops 835190784 | bytes 15728640 | tf_op jit(solution)/shard_map/qjt,qij->qit/dot_general | solution.py:62
  267.4 2.7 convolution_convert_fusion.4
  272.0 7.0 %convolution_convert_fusion.3 = bf16[24,256,256]{2,1,0:T(8,128)(2,1)} fusion(bf16[24,256,256]{2,1,0:T(8,128)(2,1)S(1)} %bitcast.80, f32[24,256,256]{2,1,0:T(8,128)} %fusion.7), kind=kOutput, calls=%fused_computation.15 | convolution fusion | flops 821035008 | bytes 12582912 | tf_op jit(solution)/shard_map/qit,qjt->qij/dot_general | solution.py:96
  280.8 2.9 convolution_convert_fusion.5
  284.2 39.5 %all_to_all.20 = bf16[1,24,4,64,256]{4,3,1,0,2:T(8,128)(2,1)S(1)} all-to-all(bf16[1,24,4,64,256]{4,3,1,0,2:T(8,128)(2,1)S(1)} %copy.48), channel_id=1, replica_groups=mesh['dp'=8,'bfly'=4] {'bfly'}, dimensions={2} | all-to-all | bytes 6291456 | tf_op jit(solution)/shard_map/all_to_all | solution.py:27
  325.0 2.7 convert_bitcast_fusion
  327.7 7.8 %copy.50 = bf16[12,256,512]{2,0,1:T(8,128)(2,1)} copy(bf16[12,256,512]{1,2,0:T(8,128)(2,1)} %convert_bitcast_fusion) | data formatting | bytes 6291456 | tf_op jit(solution)/shard_map/convert_element_type | solution.py:99
  335.6 6.6 %convolution_convert_fusion.6 = bf16[24,256,256]{1,2,0:T(8,128)(2,1)S(1)} fusion(bf16[24,256,256]{2,1,0:T(8,128)(2,1)} %all-gather.9.cloned.1.call-done, f32[24,256,256]{2,1,0:T(8,128)} %fusion.7), kind=kOutput, calls=%fused_computation.18 | convolution fusion | flops 821035008 | bytes 12582912 | tf_op jit(solution)/shard_map/qit,qij->qjt/dot_general | solution.py:82
  342.4 39.4 %all_to_all.21 = bf16[1,24,4,64,256]{4,3,1,0,2:T(8,128)(2,1)S(1)} all-to-all(bf16[1,24,4,64,256]{4,3,1,0,2:T(8,128)(2,1)S(1)} %copy.41), channel_id=1, replica_groups=mesh['dp'=8,'bfly'=4] {'bfly'}, dimensions={2} | all-to-all | bytes 6291456 | tf_op jit(solution)/shard_map/all_to_all | solution.py:27
  383.9 2.6 convolution_convert_fusion
  386.6 5.1 convolution_convert_fusion.8
  391.7 2.6 copy.53
  394.3 4.0 convolution_convert_fusion.7
  398.3 2.6 copy.54
  400.9 2.0 convert_element_type.81
  402.8 18.3 %reduce-scatter.9.cloned.1.call-done = bf16[24,32,256]{2,1,0:T(8,128)(2,1)} async-done(((bf16[24,256,256]{2,1,0:T(8,128)(2,1)}), bf16[24,32,256]{2,1,0:T(8,128)(2,1)}) %reduce-scatter.9.cloned.1.call-update) | async-done | bytes 393232 | tf_op jit(solution)/shard_map/reduce_scatter | solution.py:105
  423.1 88.9 %reduce-scatter.5.cloned.1.call-done = bf16[12,32,512]{2,0,1:T(8,128)(2,1)} async-done(((bf16[12,256,512]{2,0,1:T(8,128)(2,1)}), bf16[12,32,512]{2,0,1:T(8,128)(2,1)}) %reduce-scatter.5.cloned.1.call-update) | async-done | bytes 393232 | tf_op jit(solution)/shard_map/reduce_scatter | solution.py:99
  512.0 2.2 copy.55
  514.2 76.7 %reduce-scatter.11.cloned.1.call-done = bf16[12,64,256]{2,1,0:T(8,128)(2,1)} async-done(((bf16[12,512,256]{2,1,0:T(8,128)(2,1)}), bf16[12,64,256]{2,1,0:T(8,128)(2,1)}) %reduce-scatter.11.cloned.1.call-update) | async-done | bytes 393232 | tf_op jit(solution)/shard_map/reduce_scatter | solution.py:108
  (45 shorter events, 20.5 us)
Async XLA Ops:
  7.2 66.3 %all-gather.5.cloned.1.call-start = ((), (), s32[]{:S(2)}) async-start(), calls=%async_computation.8 | async-start | bytes 3538944 | tf_op jit(solution)/shard_map/all_gather | solution.py:37
  7.9 126.9 %all-gather.11.cloned.1.call-start = ((), (), s32[]{:S(2)}) async-start(), calls=%async_computation.11 | async-start | bytes 3538944 | tf_op jit(solution)/shard_map/all_gather | solution.py:40
  8.6 187.5 %all-gather.7.cloned.1.call-start = ((), (), s32[]{:S(2)}) async-start(), calls=%async_computation.9 | async-start | bytes 3538944 | tf_op jit(solution)/shard_map/all_gather | solution.py:38
  9.4 248.0 %all-gather.9.cloned.1.call-start = ((), (), s32[]{:S(2)}) async-start(), calls=%async_computation.10 | async-start | bytes 3538944 | tf_op jit(solution)/shard_map/all_gather | solution.py:39
  11.7 64.8 %copy-start.3 = (bf16[256,3072]{0,1:T(8,128)(2,1)}, bf16[256,3072]{0,1:T(8,128)(2,1)S(1)}, u32[]{:S(2)}) copy-start(bf16[256,3072]{0,1:T(8,128)(2,1)S(1)} %copy.36) | copy-start | bytes 4718596
  78.3 4.8 copy-start.8
  78.3 61.4 %all-to-all-start = ((bf16[1,24,4,64,256]{4,3,1,0,2:T(8,128)(2,1)}), bf16[1,24,4,64,256]{4,3,1,0,2:T(8,128)(2,1)}, u32[]{:S(2)}, u32[]{:S(2)}) async-start(bf16[1,24,4,64,256]{4,3,1,0,2:T(8,128)(2,1)} %copy.37), calls=%async_computation | async-start | bytes 6291456 | tf_op jit(solution)/shard_map/all_to_all | solution.py:27
  83.9 53.8 %copy-start.1 = (bf16[256,3072]{0,1:T(8,128)(2,1)}, bf16[256,3072]{0,1:T(8,128)(2,1)S(1)}, u32[]{:S(2)}) copy-start(bf16[256,3072]{0,1:T(8,128)(2,1)S(1)} %copy.43) | copy-start | bytes 4718596
  139.8 41.7 %all-to-all-start.2 = ((bf16[1,24,4,64,256]{4,3,1,0,2:T(8,128)(2,1)}), bf16[1,24,4,64,256]{4,3,1,0,2:T(8,128)(2,1)}, u32[]{:S(2)}, u32[]{:S(2)}) async-start(bf16[1,24,4,64,256]{4,3,1,0,2:T(8,128)(2,1)} %copy.44), calls=%async_computation.2 | async-start | bytes 6291456 | tf_op jit(solution)/shard_map/all_to_all | solution.py:27
  144.5 256.4 %reduce-scatter.7.cloned.1.call-start = ((), (), s32[]{:S(2)}) async-start(), calls=%async_computation.13 | async-start | bytes 3538944 | tf_op jit(solution)/shard_map/reduce_scatter | solution.py:102
  265.7 1.7 copy-start.6
  270.1 1.9 copy-start.7
  270.1 151.0 %reduce-scatter.9.cloned.1.call-start = ((), (), s32[]{:S(2)}) async-start(), calls=%async_computation.14 | async-start | bytes 3538944 | tf_op jit(solution)/shard_map/reduce_scatter | solution.py:105
  279.0 1.9 copy-start.5
  279.0 233.0 %reduce-scatter.5.cloned.1.call-start = ((), (), s32[]{:S(2)}) async-start(), calls=%async_computation.12 | async-start | bytes 4718592 | tf_op jit(solution)/shard_map/reduce_scatter | solution.py:99
  323.6 1.4 copy-start.4
  335.5 255.3 %reduce-scatter.11.cloned.1.call-start = ((), (), s32[]{:S(2)}) async-start(), calls=%async_computation.15 | async-start | bytes 3538944 | tf_op jit(solution)/shard_map/reduce_scatter | solution.py:108
  381.9 2.1 copy-start.2
  382.3 1.6 copy-start
Sparse Core Ops, SparseCore 0:
  10.2 63.2 all-gather.4
  75.6 59.1 all-gather.10
  137.0 59.1 all-gather.6
  198.2 59.1 all-gather.8
  270.2 73.3 reduce-scatter.6
  347.1 73.9 reduce-scatter.8
  424.8 87.2 reduce-scatter.4
  516.1 74.7 reduce-scatter.10
where the time goes:
time: 601 us; the launch traced here: 600 us
  waiting for transfers between devices  400 us (67%)
  blocking collectives  78.9 us (13%)
  matrix products  53.5 us (9%)
  local copies, waits for them, and re-layouts  36.8 us (6%)
  between operations  14.3 us (2%)
  starting transfers between devices  10 us (2%)
    reduce_scatter x1, waiting for transfers between devices, per_device(): lax.psum_scatter(part_a.astype(jnp.bfloat16), 'dp', scatter_dimension=1,...  88.9 us
    all_to_all x2, blocking collectives, regroup(): lax.all_to_all(stacked, 'bfly', split_axis=2, concat_axis=2, tiled=True)  78.9 us
    reduce_scatter x1, waiting for transfers between devices, per_device(): lax.psum_scatter(part_e.astype(jnp.bfloat16), 'dp', scatter_dimension=1,...  76.7 us
    all_gather x1, waiting for transfers between devices, per_device(): lax.all_gather(weight_a, 'dp', axis=1, tiled=True)  61.7 us
    all_gather x1, waiting for transfers between devices, per_device(): lax.all_gather(weight_c, 'dp', axis=1, tiled=True)  55.6 us
    all_gather x1, waiting for transfers between devices, per_device(): lax.all_gather(weight_e, 'dp', axis=1, tiled=True)  50.9 us
    all_to_all x2, waiting for transfers between devices, regroup(): lax.all_to_all(stacked, 'bfly', split_axis=2, concat_axis=2, tiled=True)  34.8 us
    reduce_scatter x1, waiting for transfers between devices, per_device(): lax.psum_scatter(part_c.astype(jnp.bfloat16), 'dp', scatter_dimension=1,...  18.3 us
  transfers between devices with their start and end apart: 10, of which 8 were waited for; matrix products, arithmetic and copies ran while one was open for 13% of the time, Pallas kernels for 0%

commit v1 on v0

--- a/solution.py
+++ b/solution.py
@@ -5,6 +5,22 @@
 
 BLK = 256
 gelu_scale = 0.7978845608028654
+
+
+def ring_gather(x, axis, dim):
+    ways, here, turn = (lax.axis_size(axis), lax.axis_index(axis), x.shape[dim])
+    dims = [n * ways if d == dim else n for d, n in enumerate(x.shape)]
+    full = lax.dynamic_update_slice_in_dim(jnp.zeros(dims, x.dtype), x, here * turn, axis=dim)
+    going_up = going_down = x
+    for far in range(1, ways // 2 + 1):
+        going_up = lax.ppermute(going_up, axis, [(d, (d + 1) % ways) for d in range(ways)])
+        full = lax.dynamic_update_slice_in_dim(full, going_up, (here - far) % ways * turn, axis=dim)
+        if 2 * far < ways:
+            going_down = lax.ppermute(going_down, axis, [(d, (d - 1) % ways) for d in range(ways)])
+            full = lax.dynamic_update_slice_in_dim(
+                full, going_down, (here + far) % ways * turn, axis=dim
+            )
+    return full
 
 
 def gelu_pair(hidden):
@@ -37,7 +53,7 @@
         lax.all_gather(weight_a, "dp", axis=1, tiled=True),
         lax.all_gather(weight_b, "dp", axis=1, tiled=True),
         lax.all_gather(weight_c, "dp", axis=1, tiled=True),
-        lax.all_gather(weight_e, "dp", axis=1, tiled=True),
+        ring_gather(weight_e, "dp", 1),
     )
     token_count = tokens.shape[0]
     inner_blocks = full_a.shape[0]

time: 601 us -> 575 us (0.957)
  waiting for transfers between devices: 400 us -> 355 us
  starting transfers between devices: 10 us -> 28.9 us
    ppermute x0 -> x7, waiting for transfers between devices: none -> 63.9 us  [the longest x4 61.2 us: ring_gather(): lax.ppermute(going_up, axis, [(d, (d + 1) % ways) for d in range(ways)])]
    all_gather x1, waiting for transfers between devices: 61.7 us -> 3.77 us  [per_device(): lax.all_gather(weight_a, 'dp', axis=1, tiled=True)]
    all_gather x1 -> x0, waiting for transfers between devices: 50.9 us -> none  [per_device(): lax.all_gather(weight_e, 'dp', axis=1, tiled=True)]
    all_to_all x2, waiting for transfers between devices: 34.8 us -> 60.6 us  [regroup(): lax.all_to_all(stacked, 'bfly', split_axis=2, concat_axis=2, tiled=True)]
    ppermute x0 -> x7, starting transfers between devices: none -> 19 us  [the longest x4 9.61 us: ring_gather(): lax.ppermute(going_up, axis, [(d, (d + 1) % ways) for d in range(ways)])]
    all_gather x1, waiting for transfers between devices: 55.6 us -> 41.2 us  [per_device(): lax.all_gather(weight_c, 'dp', axis=1, tiled=True)]
    all_gather x1, waiting for transfers between devices: 10.7 us -> 0.02 us  [per_device(): lax.all_gather(weight_b, 'dp', axis=1, tiled=True)]
    unnamed x23 -> x31, local copies, waits for them, and re-layouts: 17.7 us -> 19.3 us
  transfers between devices with their start and end apart: 10 -> 16, of which waited for: 8 -> 12; matrix products, arithmetic and copies ran while one was open for 13% -> 13% of each run, Pallas kernels for 0% -> 0%
where the time goes in v1:
time: 575 us; the launch traced here: 573 us
  waiting for transfers between devices  355 us (62%)
  blocking collectives  78.9 us (14%)
  matrix products  51.6 us (9%)
  local copies, waits for them, and re-layouts  38.9 us (7%)
  starting transfers between devices  28.9 us (5%)
  between operations  14.6 us (3%)
  other arithmetic  5.85 us (1%)
    reduce_scatter x1, waiting for transfers between devices, per_device(): lax.psum_scatter(part_a.astype(jnp.bfloat16), 'dp', scatter_dimension=1,...  88.7 us
    all_to_all x2, blocking collectives, regroup(): lax.all_to_all(stacked, 'bfly', split_axis=2, concat_axis=2, tiled=True)  78.9 us
    reduce_scatter x1, waiting for transfers between devices, per_device(): lax.psum_scatter(part_e.astype(jnp.bfloat16), 'dp', scatter_dimension=1,...  76.7 us
    ppermute x4, waiting for transfers between devices, ring_gather(): lax.ppermute(going_up, axis, [(d, (d + 1) % ways) for d in range(ways)])  61.2 us
    all_to_all x2, waiting for transfers between devices, regroup(): lax.all_to_all(stacked, 'bfly', split_axis=2, concat_axis=2, tiled=True)  60.6 us
    all_gather x1, waiting for transfers between devices, per_device(): lax.all_gather(weight_c, 'dp', axis=1, tiled=True)  41.2 us
    unnamed x31, local copies, waits for them, and re-layouts  19.3 us
    reduce_scatter x1, waiting for transfers between devices, per_device(): lax.psum_scatter(part_c.astype(jnp.bfloat16), 'dp', scatter_dimension=1,...  18.4 us
  transfers between devices with their start and end apart: 16, of which 12 were waited for; matrix products, arithmetic and copies ran while one was open for 13% of the time, Pallas kernels for 0%

profile of v1, /device:TPU:0, one launch (start us, length us, event | category | flops | bytes accessed | tf_op | source)
XLA Modules:
  0.0 573.5 jit_solution(5361612336812110299)
XLA Ops:
  8.7 3.0 collective-permute-start
  11.7 3.1 collective-permute-start.1
  14.8 18.2 %collective-permute-done = bf16[12,64,256]{2,1,0:T(8,128)(2,1)S(1)} collective-permute-done((bf16[12,64,256]{2,1,0:T(8,128)(2,1)}, bf16[12,64,256]{2,1,0:T(8,128)(2,1)S(1)}, u32[]{:S(2)}, u32[]{:S(2)}) %collective-permute-start) | collective-permute-done | bytes 393248 | tf_op jit(solution)/shard_map/ppermute | solution.py:16
  35.4 3.1 collective-permute-start.3
  38.5 13.6 %collective-permute-done.2 = bf16[12,64,256]{2,1,0:T(8,128)(2,1)S(1)} collective-permute-done((bf16[12,64,256]{2,1,0:T(8,128)(2,1)S(1)}, bf16[12,64,256]{2,1,0:T(8,128)(2,1)S(1)}, u32[]{:S(2)}, u32[]{:S(2)}) %collective-permute-start.2) | collective-permute-done | bytes 393248 | tf_op jit(solution)/shard_map/ppermute | solution.py:16
  57.2 3.2 collective-permute-start.5
  60.4 18.9 %collective-permute-done.4 = bf16[12,64,256]{2,1,0:T(8,128)(2,1)S(1)} collective-permute-done((bf16[12,64,256]{2,1,0:T(8,128)(2,1)S(1)}, bf16[12,64,256]{2,1,0:T(8,128)(2,1)S(1)}, u32[]{:S(2)}, u32[]{:S(2)}) %collective-permute-start.4) | collective-permute-done | bytes 393248 | tf_op jit(solution)/shard_map/ppermute | solution.py:16
  81.9 2.7 collective-permute-done.5
  84.6 10.5 %collective-permute-done.6 = bf16[12,64,256]{2,1,0:T(8,128)(2,1)S(1)} collective-permute-done((bf16[12,64,256]{2,1,0:T(8,128)(2,1)S(1)}, bf16[12,64,256]{2,1,0:T(8,128)(2,1)S(1)}, u32[]{:S(2)}, u32[]{:S(2)}) %collective-permute-start.6) | collective-permute-done | bytes 393248 | tf_op jit(solution)/shard_map/ppermute | solution.py:16
  98.9 4.8 all-to-all-start.2
  104.4 3.8 all-gather.4.cloned.1.call-done
  108.2 3.0 convolution_convert_fusion.2
  113.0 27.6 %all-to-all-done.2 = bf16[1,24,4,64,256]{4,3,1,0,2:T(8,128)(2,1)} async-done(((bf16[1,24,4,64,256]{4,3,1,0,2:T(8,128)(2,1)}), bf16[1,24,4,64,256]{4,3,1,0,2:T(8,128)(2,1)}, u32[]{:S(2)}, u32[]{:S(2)}) %all-to-all-start.2) | async-done | bytes 3145760 | tf_op jit(solution)/shard_map/all_to_all | solution.py:43
  140.7 4.6 all-to-all-start
  145.4 4.0 copy.48
  149.4 32.9 %all-to-all-done = bf16[1,24,4,64,256]{4,3,1,0,2:T(8,128)(2,1)} async-done(((bf16[1,24,4,64,256]{4,3,1,0,2:T(8,128)(2,1)}), bf16[1,24,4,64,256]{4,3,1,0,2:T(8,128)(2,1)}, u32[]{:S(2)}, u32[]{:S(2)}) %all-to-all-start) | async-done | bytes 3145760 | tf_op jit(solution)/shard_map/all_to_all | solution.py:43
  184.5 5.6 fusion.7
  190.0 41.2 %all-gather.8.cloned.1.call-done = bf16[24,256,256]{2,1,0:T(8,128)(2,1)} async-done(((bf16[24,32,256]{2,1,0:T(8,128)(2,1)}), bf16[24,256,256]{2,1,0:T(8,128)(2,1)}) %all-gather.8.cloned.1.call-update) | async-done | bytes 3145744 | tf_op jit(solution)/shard_map/all_gather | solution.py:55
  231.2 8.4 %fusion.6 = bf16[24,256,256]{1,2,0:T(8,128)(2,1)S(1)} fusion(f32[24,256,256]{2,1,0:T(8,128)} %fusion.7, bf16[24,256,256]{2,1,0:T(8,128)(2,1)} %bitcast.79, bf16[24,256,256]{2,1,0:T(8,128)(2,1)} %all-gather.8.cloned.1.call-done), kind=kOutput, calls=%fused_computation.8 | convolution fusion | flops 835190784 | bytes 15728640 | tf_op jit(solution)/shard_map/qjt,qij->qit/dot_general | solution.py:78
  241.3 2.7 convolution_convert_fusion.4
  245.9 7.0 %convolution_convert_fusion.3 = bf16[24,256,256]{2,1,0:T(8,128)(2,1)} fusion(bf16[24,256,256]{2,1,0:T(8,128)(2,1)S(1)} %bitcast.80, f32[24,256,256]{2,1,0:T(8,128)} %fusion.7), kind=kOutput, calls=%fused_computation.15 | convolution fusion | flops 821035008 | bytes 12582912 | tf_op jit(solution)/shard_map/qit,qjt->qij/dot_general | solution.py:112
  254.8 2.9 convolution_convert_fusion.5
  258.1 39.5 %all_to_all.20 = bf16[1,24,4,64,256]{4,3,1,0,2:T(8,128)(2,1)S(1)} all-to-all(bf16[1,24,4,64,256]{4,3,1,0,2:T(8,128)(2,1)S(1)} %copy.51), channel_id=1, replica_groups=mesh['dp'=8,'bfly'=4] {'bfly'}, dimensions={2} | all-to-all | bytes 6291456 | tf_op jit(solution)/shard_map/all_to_all | solution.py:43
  299.0 2.7 convert_bitcast_fusion
  301.7 7.8 %copy.53 = bf16[12,256,512]{2,0,1:T(8,128)(2,1)} copy(bf16[12,256,512]{1,2,0:T(8,128)(2,1)} %convert_bitcast_fusion) | data formatting | bytes 6291456 | tf_op jit(solution)/shard_map/convert_element_type | solution.py:115
  309.5 6.6 %convolution_convert_fusion.6 = bf16[24,256,256]{1,2,0:T(8,128)(2,1)S(1)} fusion(bf16[24,256,256]{2,1,0:T(8,128)(2,1)} %all-gather.8.cloned.1.call-done, f32[24,256,256]{2,1,0:T(8,128)} %fusion.7), kind=kOutput, calls=%fused_computation.18 | convolution fusion | flops 821035008 | bytes 12582912 | tf_op jit(solution)/shard_map/qit,qij->qjt/dot_general | solution.py:98
  316.4 39.5 %all_to_all.21 = bf16[1,24,4,64,256]{4,3,1,0,2:T(8,128)(2,1)S(1)} all-to-all(bf16[1,24,4,64,256]{4,3,1,0,2:T(8,128)(2,1)S(1)} %copy.43), channel_id=1, replica_groups=mesh['dp'=8,'bfly'=4] {'bfly'}, dimensions={2} | all-to-all | bytes 6291456 | tf_op jit(solution)/shard_map/all_to_all | solution.py:43
  360.5 5.1 convolution_convert_fusion.8
  368.2 4.0 convolution_convert_fusion.7
  376.8 18.4 %reduce-scatter.9.cloned.1.call-done = bf16[24,32,256]{2,1,0:T(8,128)(2,1)} async-done(((bf16[24,256,256]{2,1,0:T(8,128)(2,1)}), bf16[24,32,256]{2,1,0:T(8,128)(2,1)}) %reduce-scatter.9.cloned.1.call-update) | async-done | bytes 393232 | tf_op jit(solution)/shard_map/reduce_scatter | solution.py:121
  397.1 88.7 %reduce-scatter.5.cloned.1.call-done = bf16[12,32,512]{2,0,1:T(8,128)(2,1)} async-done(((bf16[12,256,512]{2,0,1:T(8,128)(2,1)}), bf16[12,32,512]{2,0,1:T(8,128)(2,1)}) %reduce-scatter.5.cloned.1.call-update) | async-done | bytes 393232 | tf_op jit(solution)/shard_map/reduce_scatter | solution.py:115
  488.0 76.7 %reduce-scatter.11.cloned.1.call-done = bf16[12,64,256]{2,1,0:T(8,128)(2,1)} async-done(((bf16[12,512,256]{2,1,0:T(8,128)(2,1)}), bf16[12,64,256]{2,1,0:T(8,128)(2,1)}) %reduce-scatter.11.cloned.1.call-update) | async-done | bytes 393232 | tf_op jit(solution)/shard_map/reduce_scatter | solution.py:124
  (73 shorter events, 45.1 us)
Async XLA Ops:
  7.2 101.0 %all-gather.4.cloned.1.call-start = ((), (), s32[]{:S(2)}) async-start(), calls=%async_computation.8 | async-start | bytes 3538944 | tf_op jit(solution)/shard_map/all_gather | solution.py:53
  7.9 176.6 %all-gather.6.cloned.1.call-start = ((), (), s32[]{:S(2)}) async-start(), calls=%async_computation.9 | async-start | bytes 3538944 | tf_op jit(solution)/shard_map/all_gather | solution.py:54
  8.6 222.6 %all-gather.8.cloned.1.call-start = ((), (), s32[]{:S(2)}) async-start(), calls=%async_computation.10 | async-start | bytes 3538944 | tf_op jit(solution)/shard_map/all_gather | solution.py:55
  8.7 24.3 %collective-permute-start = (bf16[12,64,256]{2,1,0:T(8,128)(2,1)}, bf16[12,64,256]{2,1,0:T(8,128)(2,1)S(1)}, u32[]{:S(2)}, u32[]{:S(2)}) collective-permute-start(bf16[12,64,256]{2,1,0:T(8,128)(2,1)} %param.11), channel_id=1, source_target_pairs={{0,4},{4,8},{8,12},{12,16},{16,20},{20,24},{24,28},{28,0},{1,5},{5... | collective-permute-start | bytes 1179656 | tf_op jit(solution)/shard_map/ppermute | solution.py:16
  11.7 23.7 %collective-permute-start.1 = (bf16[12,64,256]{2,1,0:T(8,128)(2,1)}, bf16[12,64,256]{2,1,0:T(8,128)(2,1)S(1)}, u32[]{:S(2)}, u32[]{:S(2)}) collective-permute-start(bf16[12,64,256]{2,1,0:T(8,128)(2,1)} %param.11), channel_id=1, source_target_pairs={{0,28},{4,0},{8,4},{12,8},{16,12},{20,16},{24,20},{28,24},{1,29},{... | collective-permute-start | bytes 1179656 | tf_op jit(solution)/shard_map/ppermute | solution.py:19
  33.0 19.1 %copy-start.11 = (bf16[12,64,256]{2,1,0:T(8,128)(2,1)}, bf16[12,64,256]{2,1,0:T(8,128)(2,1)S(1)}, u32[]{:S(2)}) copy-start(bf16[12,64,256]{2,1,0:T(8,128)(2,1)S(1)} %collective-permute-done) | copy-start | bytes 1179652
  33.0 19.1 %collective-permute-start.2 = (bf16[12,64,256]{2,1,0:T(8,128)(2,1)S(1)}, bf16[12,64,256]{2,1,0:T(8,128)(2,1)S(1)}, u32[]{:S(2)}, u32[]{:S(2)}) collective-permute-start(bf16[12,64,256]{2,1,0:T(8,128)(2,1)S(1)} %collective-permute-done), channel_id=1, source_target_pairs={{0,4},{4,8},{8,12},{12,16},{16,20},{20,24},{24,28},{28,0},{1,5},{5... | collective-permute-start | bytes 1179656 | tf_op jit(solution)/shard_map/ppermute | solution.py:16
  35.4 21.8 %collective-permute-start.3 = (bf16[12,64,256]{2,1,0:T(8,128)(2,1)S(1)}, bf16[12,64,256]{2,1,0:T(8,128)(2,1)S(1)}, u32[]{:S(2)}, u32[]{:S(2)}) collective-permute-start(bf16[12,64,256]{2,1,0:T(8,128)(2,1)S(1)} %collective-permute-done.1), channel_id=1, source_target_pairs={{0,28},{4,0},{8,4},{12,8},{16,12},{20,16},{24,20},{28,24},{1,29},{... | collective-permute-start | bytes 1179656 | tf_op jit(solution)/shard_map/ppermute | solution.py:19
  52.1 27.1 %collective-permute-start.4 = (bf16[12,64,256]{2,1,0:T(8,128)(2,1)S(1)}, bf16[12,64,256]{2,1,0:T(8,128)(2,1)S(1)}, u32[]{:S(2)}, u32[]{:S(2)}) collective-permute-start(bf16[12,64,256]{2,1,0:T(8,128)(2,1)S(1)} %collective-permute-done.2), channel_id=1, source_target_pairs={{0,4},{4,8},{8,12},{12,16},{16,20},{20,24},{24,28},{28,0},{1,5},{5... | collective-permute-start | bytes 1179656 | tf_op jit(solution)/shard_map/ppermute | solution.py:16
  54.0 2.1 copy-start.10
  55.8 39.4 %copy-start.2 = (bf16[256,3072]{0,1:T(8,128)(2,1)}, bf16[256,3072]{0,1:T(8,128)(2,1)S(1)}, u32[]{:S(2)}) copy-start(bf16[256,3072]{0,1:T(8,128)(2,1)S(1)} %copy.46) | copy-start | bytes 4718596
  55.9 1.3 copy-start.12
  57.2 27.4 %collective-permute-start.5 = (bf16[12,64,256]{2,1,0:T(8,128)(2,1)S(1)}, bf16[12,64,256]{2,1,0:T(8,128)(2,1)S(1)}, u32[]{:S(2)}, u32[]{:S(2)}) collective-permute-start(bf16[12,64,256]{2,1,0:T(8,128)(2,1)S(1)} %collective-permute-done.3), channel_id=1, source_target_pairs={{0,28},{4,0},{8,4},{12,8},{16,12},{20,16},{24,20},{28,24},{1,29},{... | collective-permute-start | bytes 1179656 | tf_op jit(solution)/shard_map/ppermute | solution.py:19
  79.3 15.8 %collective-permute-start.6 = (bf16[12,64,256]{2,1,0:T(8,128)(2,1)S(1)}, bf16[12,64,256]{2,1,0:T(8,128)(2,1)S(1)}, u32[]{:S(2)}, u32[]{:S(2)}) collective-permute-start(bf16[12,64,256]{2,1,0:T(8,128)(2,1)S(1)} %collective-permute-done.4), channel_id=1, source_target_pairs={{0,4},{4,8},{8,12},{12,16},{16,20},{20,24},{24,28},{28,0},{1,5},{5... | collective-permute-start | bytes 1179656 | tf_op jit(solution)/shard_map/ppermute | solution.py:16
  95.1 1.6 copy-start.1
  98.9 4.8 copy-start.9
  98.9 41.8 %all-to-all-start.2 = ((bf16[1,24,4,64,256]{4,3,1,0,2:T(8,128)(2,1)}), bf16[1,24,4,64,256]{4,3,1,0,2:T(8,128)(2,1)}, u32[]{:S(2)}, u32[]{:S(2)}) async-start(bf16[1,24,4,64,256]{4,3,1,0,2:T(8,128)(2,1)} %copy.47), calls=%async_computation.2 | async-start | bytes 6291456 | tf_op jit(solution)/shard_map/all_to_all | solution.py:43
  104.4 6.8 %copy-start.4 = (bf16[256,3072]{0,1:T(8,128)(2,1)}, bf16[256,3072]{0,1:T(8,128)(2,1)S(1)}, u32[]{:S(2)}) copy-start(bf16[256,3072]{0,1:T(8,128)(2,1)S(1)} %copy.38) | copy-start | bytes 4718596
  140.7 41.6 %all-to-all-start = ((bf16[1,24,4,64,256]{4,3,1,0,2:T(8,128)(2,1)}), bf16[1,24,4,64,256]{4,3,1,0,2:T(8,128)(2,1)}, u32[]{:S(2)}, u32[]{:S(2)}) async-start(bf16[1,24,4,64,256]{4,3,1,0,2:T(8,128)(2,1)} %copy.39), calls=%async_computation | async-start | bytes 6291456 | tf_op jit(solution)/shard_map/all_to_all | solution.py:43
  145.3 229.5 %reduce-scatter.7.cloned.1.call-start = ((), (), s32[]{:S(2)}) async-start(), calls=%async_computation.12 | async-start | bytes 3538944 | tf_op jit(solution)/shard_map/reduce_scatter | solution.py:118
  239.6 1.7 copy-start.7
  244.0 1.9 copy-start.8
  244.0 151.2 %reduce-scatter.9.cloned.1.call-start = ((), (), s32[]{:S(2)}) async-start(), calls=%async_computation.13 | async-start | bytes 3538944 | tf_op jit(solution)/shard_map/reduce_scatter | solution.py:121
  252.9 1.9 copy-start.6
  252.9 232.9 %reduce-scatter.5.cloned.1.call-start = ((), (), s32[]{:S(2)}) async-start(), calls=%async_computation.11 | async-start | bytes 4718592 | tf_op jit(solution)/shard_map/reduce_scatter | solution.py:115
  297.6 1.4 copy-start.5
  309.5 255.2 %reduce-scatter.11.cloned.1.call-start = ((), (), s32[]{:S(2)}) async-start(), calls=%async_computation.14 | async-start | bytes 3538944 | tf_op jit(solution)/shard_map/reduce_scatter | solution.py:124
  355.8 2.1 copy-start.3
  356.2 1.6 copy-start
Sparse Core Ops, SparseCore 0:
  10.2 97.9 all-gather.3
  110.3 59.4 all-gather.5
  172.1 59.1 all-gather.7
  244.1 73.5 reduce-scatter.6
  321.2 73.9 reduce-scatter.8
  398.7 87.1 reduce-scatter.4
  489.9 74.7 reduce-scatter.10
